TPU v7x, 128 devices: a whole 4x4x4 slice. The times are simulated.
128 devices in a mesh: seq: 16 (over x, y_hi, core), fsdp: 8 (over z, y_lo).
Axes of the slice: x: 4, y: 4 (y_hi: 2, y_lo: 2; y = y_hi * 2 + y_lo), z: 4, core: 2. Of those that a mesh axis runs over, the one named last changes fastest.
Arguments:
- normed: bfloat16 [131072, 1024], P(('seq', 'fsdp')), may hold values from -31 to 31, as said below
- w_qkv: bfloat16 [1024, 3072], P('fsdp'), may hold values from -0.5 to 0.5, as said below
- w_out: bfloat16 [1024, 1024], P('fsdp'), may hold values from -0.5 to 0.5
- layout: int32 [1024, 10], P(('seq', 'fsdp')), may hold values from 0 to 23, as said below
- counts: int32 [1024], P(('seq', 'fsdp')), may hold values from 1 to 10, as said below
Outputs:
- mixed: bfloat16 [131072, 1024], P(('seq', 'fsdp'))
Inputs may be any that keep to these rules, and one draw needn't show every extreme that they name: `normed`: float activations. `w_qkv`: float weights. `layout`: each row holds 10 distinct pool entries, never the query block's own entry; entries 0 to 7 name the blocks of the station one step lower along seq, the last 8 those one step higher. `counts`: the value 10 occurs in every draw.
All inputs are finite; a program needn't handle non-finite values.
Results may differ from a plain program's by a relative error of at most 0.0099.
Values may be sent and summed in bfloat16 or wider, within the bound.
A program may use at most 128 MiB of HBM per device.

v0:
```python
import math
import jax
import jax.numpy as jnp
from jax import lax
from jax.sharding import PartitionSpec as P

HEADS = 8
BLOCK = 128
KEY_BLOCKS = 10


def from_behind(value, axis, steps):
    count = lax.axis_size(axis)
    pairs = [(source, (source + steps) % count) for source in range(count)]
    return lax.ppermute(value, axis, pairs)


def attend(query, own_blocks, picked, used):
    block_count = picked.shape[0]
    feature_width = query.shape[1]
    head_width = feature_width // HEADS
    keyvals = jnp.concatenate([own_blocks[:, None], picked], axis=1)
    keyvals = keyvals.reshape(block_count, (KEY_BLOCKS + 1) * BLOCK, 2 * feature_width)
    key_heads = keyvals[..., :feature_width].reshape(block_count, -1, HEADS, head_width)
    value_heads = keyvals[..., feature_width:].reshape(block_count, -1, HEADS, head_width)
    query_heads = query.reshape(block_count, BLOCK, HEADS, head_width)
    scores = jnp.einsum(
        "bqhd,bkhd->bhqk", query_heads, key_heads, preferred_element_type=jnp.float32
    )
    scores = scores * head_width ** (-0.5)
    slot_number = jnp.arange((KEY_BLOCKS + 1) * BLOCK, dtype=jnp.int32) // BLOCK
    usable = slot_number[None, :] <= used[:, None]
    scores = jnp.where(usable[:, None, None, :], scores, -jnp.inf)
    largest = jnp.max(scores, axis=-1, keepdims=True)
    expons = jnp.exp(scores - largest)
    denominator = jnp.sum(expons, axis=-1, keepdims=True)
    rounded = expons.astype(jnp.bfloat16)
    summed = jnp.einsum("bhqk,bkhd->bqhd", rounded, value_heads, preferred_element_type=jnp.float32)
    summed = summed / jnp.transpose(denominator, (0, 2, 1, 3))
    return summed.reshape(block_count * BLOCK, feature_width).astype(jnp.bfloat16)


def shards(normed, w_qkv, w_out, layout, counts):
    row_count, feature_width = normed.shape
    blocks_here = row_count // BLOCK
    sources = (normed,)
    start_sums = [jnp.zeros((row_count, 3 * feature_width), jnp.float32)]
    start_sums = tuple(start_sums)
    own_cols = sources[0]
    fresh = [
        jnp.dot(
            own_cols,
            lax.all_gather(w_qkv, "fsdp", axis=0, tiled=True),
            preferred_element_type=jnp.float32,
        )
    ]
    sums = tuple(fresh)
    packed = sums[0].astype(jnp.bfloat16)
    queries = packed[:, :feature_width]
    keyvals = packed[:, feature_width:]
    lower_keys = from_behind(keyvals, "seq", 1)
    upper_keys = from_behind(keyvals, "seq", -1)
    pool_rows = jnp.concatenate([lower_keys, keyvals, upper_keys], axis=0)
    pool = pool_rows.reshape(3 * blocks_here, BLOCK, 2 * feature_width)
    group_size = math.gcd(blocks_here, max(1, 256 // BLOCK))
    group_count = blocks_here // group_size

    def one_group(items):
        query_part, layout_part, count_part, group_number = items
        own_blocks = lax.dynamic_slice_in_dim(
            pool, blocks_here + group_number * group_size, group_size, 0
        )
        picked = pool[layout_part]
        return attend(query_part, own_blocks, picked, count_part)

    attended = lax.map(
        one_group,
        (
            queries.reshape(group_count, group_size * BLOCK, feature_width),
            layout.reshape(group_count, group_size, KEY_BLOCKS),
            counts.reshape(group_count, group_size),
            jnp.arange(group_count, dtype=jnp.int32),
        ),
    )
    attended = attended.reshape(row_count, feature_width)
    output_sum = jnp.dot(
        attended,
        lax.all_gather(w_out, "fsdp", axis=0, tiled=True),
        preferred_element_type=jnp.float32,
    )
    return output_sum.astype(jnp.bfloat16)


def solution(mesh):
    return jax.shard_map(
        shards,
        mesh=mesh,
        in_specs=(
            P(("seq", "fsdp"), None),
            P("fsdp", None),
            P("fsdp", None),
            P(("seq", "fsdp"), None),
            P(("seq", "fsdp")),
        ),
        out_specs=P(("seq", "fsdp"), None),
        check_vma=False,
    )
```

profile of v0, /device:TPU:1, one launch (start us, length us, event | category | flops | bytes accessed | tf_op | source)
XLA Modules:
  0.0 604.0 jit_solution(1905112295235655145)
XLA Ops:
  7.3 134.3 %all-gather.3.cloned.1.call-done = bf16[1024,3072]{1,0:T(8,128)(2,1)} async-done(((bf16[128,3072]{1,0:T(8,128)(2,1)}), bf16[1024,3072]{1,0:T(8,128)(2,1)}) %all-gather.3.cloned.1.call-update) | async-done | bytes 6291472 | tf_op jit(solution)/shard_map/all_gather | solution.py:53
  141.6 9.6 %convolution_convert_fusion = bf16[1024,3072]{1,0:T(8,128)(2,1)S(1)} fusion(bf16[1024,1024]{1,0:T(8,128)(2,1)S(1)} %copy-done, bf16[1024,3072]{1,0:T(8,128)(2,1)} %all-gather.3.cloned.1.call-done), kind=kOutput, calls=%fused_computation.36 | convolution fusion | flops 6445596672 | bytes 14680064 | tf_op jit(solution)/shard_map/dot_general | solution.py:51
  162.6 126.8 %collective-permute-done = bf16[1024,2048]{1,0:T(8,128)(2,1)} collective-permute-done((bf16[1024,2048]{1,0:T(8,128)(2,1)}, bf16[1024,2048]{1,0:T(8,128)(2,1)}, u32[]{:S(2)}, u32[]{:S(2)}) %collective-permute-start) | collective-permute-done | bytes 4194336 | tf_op jit(solution)/shard_map/ppermute | solution.py:15
  292.5 11.4 %pad_maximum_fusion.1 = bf16[3072,2048]{1,0:T(8,128)(2,1)} fusion(bf16[1024,2048]{1,0:T(8,128)(2,1)} %collective-permute-done.1, bf16[1024,2048]{1,0:T(8,128)(2,1)} %slice.24, bf16[1024,2048]{1,0:T(8,128)(2,1)} %collective-permute-done), kind=kLoop, calls=%fused_computation.35 | loop fusion | flops 37748736 | bytes 25165824 | tf_op jit(solution)/shard_map/concatenate | solution.py:63
  303.9 287.3 %while.12 = (s32[]{:T(128)}, bf16[4,256,1024]{2,1,0:T(8,128)(2,1)}, s32[4]{0:T(128)S(1)}, bf16[24,128,2048]{2,1,0:T(8,128)(2,1)}, s32[4,2,10]{2,1,0:T(2,128)}, /...) while((s32[]{:T(128)}, bf16[4,256,1024]{2,1,0:T(8,128)(2,1)}, ...), condition=%wide.region_3.4_spmd, body=%wide.region_0.3_spmd.sunk | while | flops 1514416896 | bytes 190909680 | solution.py:76
  307.1 10.0 %gather_fusion = bf16[20,128,2048]{2,1,0:T(8,128)(2,1)} fusion(bf16[24,128,2048]{2,1,0:T(8,128)(2,1)} %get-tuple-element.200, s32[1024]{0:T(1024)S(1)} %pad_clamp_fusion.2), kind=kCustom, calls=%fused_computation.clone.1 | custom fusion | bytes 20971600 | tf_op jit(solution)/shard_map/while/body/eval_jaxpr/gather | solution.py:73
  317.1 10.1 %pad_maximum_fusion.3 = bf16[2,11,128,2048]{3,2,1,0:T(8,128)(2,1)} fusion(bf16[2,10,128,2048]{3,2,1,0:T(8,128)(2,1)} %bitcast.74, bf16[2,1,128,2048]{3,2,1,0:T(8,128)(2,1)S(1)} %dynamic-slice_bitcast_fusion.4), kind=kLoop, calls=%fused_computation.1.clone.1 | loop fusion | flops 5767168 | bytes 23068672 | tf_op jit(solution)/shard_map/while/body/eval_jaxpr/concatenate | solution.py:22
  327.2 9.9 %fusion.40 = (bf16[2,1408,1024]{2,1,0:T(8,128)(2,1)}, bf16[2,1408,1024]{2,1,0:T(8,128)(2,1)}) fusion(bf16[2,1408,2048]{2,1,0:T(8,128)(2,1)} %bitcast.72), kind=kLoop, calls=%fused_computation.38.clone.1 | loop fusion | bytes 23068672 | tf_op jit(solution)/shard_map/while/body/eval_jaxpr/slice | solution.py:24
  337.1 8.3 %copy.26 = bf16[2,1408,1024]{1,2,0:T(8,128)(2,1)} copy(bf16[2,1408,1024]{2,1,0:T(8,128)(2,1)} %get-tuple-element.170) | data formatting | bytes 11534336 | tf_op jit(solution)/shard_map/while/body/eval_jaxpr/slice | solution.py:24
  350.5 4.2 copy-done.2
  357.1 8.4 %copy.25 = bf16[2,1408,1024]{1,2,0:T(8,128)(2,1)} copy(bf16[2,1408,1024]{2,1,0:T(8,128)(2,1)} %get-tuple-element.169) | data formatting | bytes 11534336 | tf_op jit(solution)/shard_map/while/body/eval_jaxpr/slice | solution.py:25
  365.5 8.8 %divide_convert_fusion.2 = bf16[2,128,8,128]{1,3,2,0:T(8,128)(2,1)S(1)} fusion(bf16[2,1408,8,128]{1,3,2,0:T(8,128)(2,1)} %bitcast.76, f32[2,8,128,1408]{3,2,1,0:T(8,128)} %copy-done.2, f32[2,8,128]{2,1,0:T(8,128)S(1)} %get-tuple-element.172, pred[2,1408]{1,0:T(4,128)(4,1)S(1)} %broadcast_compare_fusion.2, f32[2,128,8]{1,2,0:T(8,128)S(1)} %bitcast.79), kind=kOutput, calls=%fused_computation.13.clone.1 | convolution fusion | flops 750256128 | bytes 17844992 | tf_op jit(solution)/shard_map/while/body/eval_jaxpr/bhqk,bkhd->bqhd/dot_general | solution.py:38
  378.9 10.0 %gather_fusion = bf16[20,128,2048]{2,1,0:T(8,128)(2,1)} fusion(bf16[24,128,2048]{2,1,0:T(8,128)(2,1)} %get-tuple-element.200, s32[1024]{0:T(1024)S(1)} %pad_clamp_fusion.2), kind=kCustom, calls=%fused_computation.clone.1 | custom fusion | bytes 20971600 | tf_op jit(solution)/shard_map/while/body/eval_jaxpr/gather | solution.py:73
  388.9 10.1 %pad_maximum_fusion.3 = bf16[2,11,128,2048]{3,2,1,0:T(8,128)(2,1)} fusion(bf16[2,10,128,2048]{3,2,1,0:T(8,128)(2,1)} %bitcast.74, bf16[2,1,128,2048]{3,2,1,0:T(8,128)(2,1)S(1)} %dynamic-slice_bitcast_fusion.4), kind=kLoop, calls=%fused_computation.1.clone.1 | loop fusion | flops 5767168 | bytes 23068672 | tf_op jit(solution)/shard_map/while/body/eval_jaxpr/concatenate | solution.py:22
  399.0 9.9 %fusion.40 = (bf16[2,1408,1024]{2,1,0:T(8,128)(2,1)}, bf16[2,1408,1024]{2,1,0:T(8,128)(2,1)}) fusion(bf16[2,1408,2048]{2,1,0:T(8,128)(2,1)} %bitcast.72), kind=kLoop, calls=%fused_computation.38.clone.1 | loop fusion | bytes 23068672 | tf_op jit(solution)/shard_map/while/body/eval_jaxpr/slice | solution.py:24
  408.9 8.3 %copy.26 = bf16[2,1408,1024]{1,2,0:T(8,128)(2,1)} copy(bf16[2,1408,1024]{2,1,0:T(8,128)(2,1)} %get-tuple-element.170) | data formatting | bytes 11534336 | tf_op jit(solution)/shard_map/while/body/eval_jaxpr/slice | solution.py:24
  422.4 4.2 copy-done.2
  428.9 8.4 %copy.25 = bf16[2,1408,1024]{1,2,0:T(8,128)(2,1)} copy(bf16[2,1408,1024]{2,1,0:T(8,128)(2,1)} %get-tuple-element.169) | data formatting | bytes 11534336 | tf_op jit(solution)/shard_map/while/body/eval_jaxpr/slice | solution.py:25
  437.3 8.8 %divide_convert_fusion.2 = bf16[2,128,8,128]{1,3,2,0:T(8,128)(2,1)S(1)} fusion(bf16[2,1408,8,128]{1,3,2,0:T(8,128)(2,1)} %bitcast.76, f32[2,8,128,1408]{3,2,1,0:T(8,128)} %copy-done.2, f32[2,8,128]{2,1,0:T(8,128)S(1)} %get-tuple-element.172, pred[2,1408]{1,0:T(4,128)(4,1)S(1)} %broadcast_compare_fusion.2, f32[2,128,8]{1,2,0:T(8,128)S(1)} %bitcast.79), kind=kOutput, calls=%fused_computation.13.clone.1 | convolution fusion | flops 750256128 | bytes 17844992 | tf_op jit(solution)/shard_map/while/body/eval_jaxpr/bhqk,bkhd->bqhd/dot_general | solution.py:38
  450.8 10.0 %gather_fusion = bf16[20,128,2048]{2,1,0:T(8,128)(2,1)} fusion(bf16[24,128,2048]{2,1,0:T(8,128)(2,1)} %get-tuple-element.200, s32[1024]{0:T(1024)S(1)} %pad_clamp_fusion.2), kind=kCustom, calls=%fused_computation.clone.1 | custom fusion | bytes 20971600 | tf_op jit(solution)/shard_map/while/body/eval_jaxpr/gather | solution.py:73
  460.8 10.1 %pad_maximum_fusion.3 = bf16[2,11,128,2048]{3,2,1,0:T(8,128)(2,1)} fusion(bf16[2,10,128,2048]{3,2,1,0:T(8,128)(2,1)} %bitcast.74, bf16[2,1,128,2048]{3,2,1,0:T(8,128)(2,1)S(1)} %dynamic-slice_bitcast_fusion.4), kind=kLoop, calls=%fused_computation.1.clone.1 | loop fusion | flops 5767168 | bytes 23068672 | tf_op jit(solution)/shard_map/while/body/eval_jaxpr/concatenate | solution.py:22
  470.8 9.9 %fusion.40 = (bf16[2,1408,1024]{2,1,0:T(8,128)(2,1)}, bf16[2,1408,1024]{2,1,0:T(8,128)(2,1)}) fusion(bf16[2,1408,2048]{2,1,0:T(8,128)(2,1)} %bitcast.72), kind=kLoop, calls=%fused_computation.38.clone.1 | loop fusion | bytes 23068672 | tf_op jit(solution)/shard_map/while/body/eval_jaxpr/slice | solution.py:24
  480.8 8.3 %copy.26 = bf16[2,1408,1024]{1,2,0:T(8,128)(2,1)} copy(bf16[2,1408,1024]{2,1,0:T(8,128)(2,1)} %get-tuple-element.170) | data formatting | bytes 11534336 | tf_op jit(solution)/shard_map/while/body/eval_jaxpr/slice | solution.py:24
  500.8 8.4 %copy.25 = bf16[2,1408,1024]{1,2,0:T(8,128)(2,1)} copy(bf16[2,1408,1024]{2,1,0:T(8,128)(2,1)} %get-tuple-element.169) | data formatting | bytes 11534336 | tf_op jit(solution)/shard_map/while/body/eval_jaxpr/slice | solution.py:25
  509.2 8.8 %divide_convert_fusion.2 = bf16[2,128,8,128]{1,3,2,0:T(8,128)(2,1)S(1)} fusion(bf16[2,1408,8,128]{1,3,2,0:T(8,128)(2,1)} %bitcast.76, f32[2,8,128,1408]{3,2,1,0:T(8,128)} %copy-done.2, f32[2,8,128]{2,1,0:T(8,128)S(1)} %get-tuple-element.172, pred[2,1408]{1,0:T(4,128)(4,1)S(1)} %broadcast_compare_fusion.2, f32[2,128,8]{1,2,0:T(8,128)S(1)} %bitcast.79), kind=kOutput, calls=%fused_computation.13.clone.1 | convolution fusion | flops 750256128 | bytes 17844992 | tf_op jit(solution)/shard_map/while/body/eval_jaxpr/bhqk,bkhd->bqhd/dot_general | solution.py:38
  522.6 10.0 %gather_fusion = bf16[20,128,2048]{2,1,0:T(8,128)(2,1)} fusion(bf16[24,128,2048]{2,1,0:T(8,128)(2,1)} %get-tuple-element.200, s32[1024]{0:T(1024)S(1)} %pad_clamp_fusion.2), kind=kCustom, calls=%fused_computation.clone.1 | custom fusion | bytes 20971600 | tf_op jit(solution)/shard_map/while/body/eval_jaxpr/gather | solution.py:73
  532.6 10.1 %pad_maximum_fusion.3 = bf16[2,11,128,2048]{3,2,1,0:T(8,128)(2,1)} fusion(bf16[2,10,128,2048]{3,2,1,0:T(8,128)(2,1)} %bitcast.74, bf16[2,1,128,2048]{3,2,1,0:T(8,128)(2,1)S(1)} %dynamic-slice_bitcast_fusion.4), kind=kLoop, calls=%fused_computation.1.clone.1 | loop fusion | flops 5767168 | bytes 23068672 | tf_op jit(solution)/shard_map/while/body/eval_jaxpr/concatenate | solution.py:22
  542.7 9.9 %fusion.40 = (bf16[2,1408,1024]{2,1,0:T(8,128)(2,1)}, bf16[2,1408,1024]{2,1,0:T(8,128)(2,1)}) fusion(bf16[2,1408,2048]{2,1,0:T(8,128)(2,1)} %bitcast.72), kind=kLoop, calls=%fused_computation.38.clone.1 | loop fusion | bytes 23068672 | tf_op jit(solution)/shard_map/while/body/eval_jaxpr/slice | solution.py:24
  552.6 8.3 %copy.26 = bf16[2,1408,1024]{1,2,0:T(8,128)(2,1)} copy(bf16[2,1408,1024]{2,1,0:T(8,128)(2,1)} %get-tuple-element.170) | data formatting | bytes 11534336 | tf_op jit(solution)/shard_map/while/body/eval_jaxpr/slice | solution.py:24
  572.6 8.4 %copy.25 = bf16[2,1408,1024]{1,2,0:T(8,128)(2,1)} copy(bf16[2,1408,1024]{2,1,0:T(8,128)(2,1)} %get-tuple-element.169) | data formatting | bytes 11534336 | tf_op jit(solution)/shard_map/while/body/eval_jaxpr/slice | solution.py:25
  581.0 8.8 %divide_convert_fusion.2 = bf16[2,128,8,128]{1,3,2,0:T(8,128)(2,1)S(1)} fusion(bf16[2,1408,8,128]{1,3,2,0:T(8,128)(2,1)} %bitcast.76, f32[2,8,128,1408]{3,2,1,0:T(8,128)} %copy-done.2, f32[2,8,128]{2,1,0:T(8,128)S(1)} %get-tuple-element.172, pred[2,1408]{1,0:T(4,128)(4,1)S(1)} %broadcast_compare_fusion.2, f32[2,128,8]{1,2,0:T(8,128)S(1)} %bitcast.79), kind=kOutput, calls=%fused_computation.13.clone.1 | convolution fusion | flops 750256128 | bytes 17844992 | tf_op jit(solution)/shard_map/while/body/eval_jaxpr/bhqk,bkhd->bqhd/dot_general | solution.py:38
  591.2 6.0 convolution_convert_fusion.1
  (87 shorter events, 69.8 us)
Async XLA Ops:
  6.5 135.1 %copy-start = (bf16[1024,1024]{1,0:T(8,128)(2,1)S(1)}, bf16[1024,1024]{1,0:T(8,128)(2,1)}, u32[]{:S(2)}) copy-start(bf16[1024,1024]{1,0:T(8,128)(2,1)} %param.7) | copy-start | bytes 6291460
  6.5 135.1 %all-gather.3.cloned.1.call-start = ((), (), s32[]{:S(2)}) async-start(), calls=%async_computation | async-start | bytes 7077888 | tf_op jit(solution)/shard_map/all_gather | solution.py:53
  7.3 583.9 %all-gather.5.cloned.1.call-start = ((), (), s32[]{:S(2)}) async-start(), calls=%async_computation.1 | async-start | bytes 2359296 | tf_op jit(solution)/shard_map/all_gather | solution.py:88
  151.3 2.7 copy-start.3
  153.9 5.5 copy-start.4
  156.2 133.3 %collective-permute-start = (bf16[1024,2048]{1,0:T(8,128)(2,1)}, bf16[1024,2048]{1,0:T(8,128)(2,1)}, u32[]{:S(2)}, u32[]{:S(2)}) collective-permute-start(bf16[1024,2048]{1,0:T(8,128)(2,1)} %slice.24), channel_id=1, source_target_pairs={{0,8},{8,16},{16,24},{24,32},{32,40},{40,48},{48,56},{56,64},{64,7... | collective-permute-start | bytes 12582920 | tf_op jit(solution)/shard_map/ppermute | solution.py:15
  159.4 133.1 %collective-permute-start.1 = (bf16[1024,2048]{1,0:T(8,128)(2,1)}, bf16[1024,2048]{1,0:T(8,128)(2,1)}, u32[]{:S(2)}, u32[]{:S(2)}) collective-permute-start(bf16[1024,2048]{1,0:T(8,128)(2,1)} %slice.24), channel_id=1, source_target_pairs={{0,120},{8,0},{16,8},{24,16},{32,24},{40,32},{48,40},{56,48},{64,5... | collective-permute-start | bytes 12582920 | tf_op jit(solution)/shard_map/ppermute | solution.py:15
  350.5 4.2 copy-start.2
  422.3 4.2 copy-start.2
  494.2 4.2 copy-start.2
  566.0 4.2 copy-start.2
  591.2 6.0 copy-start.1
Sparse Core Ops, SparseCore 0:
  9.0 132.5 all-gather.2
  159.5 109.6 all-gather.4
where the time goes:
time: 607 us; the launch traced here: 604 us
  waiting for transfers between devices  265 us (44%)
  local copies, waits for them, and re-layouts  189 us (31%)
  matrix products  66.5 us (11%)
  other arithmetic  64.4 us (11%)
  between operations  13.4 us (2%)
    all_gather x1, waiting for transfers between devices, shards(): lax.all_gather(w_qkv, 'fsdp', axis=0, tiled=True)  134 us
    ppermute x2, waiting for transfers between devices, from_behind(): return lax.ppermute(value, axis, pairs)  130 us
    slice x8, local copies, waits for them, and re-layouts, attend(): keyvals[..., :feature_width].reshape(block_count, -1, HEADS, head_width)  72.8 us
    concatenate x4, other arithmetic, attend(): keyvals = jnp.concatenate([own_blocks[:, None], picked], axis=1)  40.2 us
    gather x4, local copies, waits for them, and re-layouts, one_group(): picked = pool[layout_part]  40 us
    dot_general x4, matrix products, attend(): jnp.einsum('bhqk,bkhd->bqhd', rounded, value_heads, preferred_element_typ...  35.3 us
    slice x4, local copies, waits for them, and re-layouts, attend(): keyvals[..., feature_width:].reshape(block_count, -1, HEADS, head_width)  33.5 us
    while x16, local copies, waits for them, and re-layouts  21.4 us
  transfers between devices with their start and end apart: 4, of which 3 were waited for; matrix products, arithmetic and copies ran while one was open for 47% of the time, Pallas kernels for 0%

commit v1 on v0

--- a/solution.py
+++ b/solution.py
@@ -7,6 +7,11 @@
 HEADS = 8
 BLOCK = 128
 KEY_BLOCKS = 10
+
+
+def gather_over(x, axis, dim):
+    sent = jnp.stack([x] * lax.axis_size(axis))
+    return jnp.concatenate(lax.all_to_all(sent, axis, 0, 0), axis=dim)
 
 
 def from_behind(value, axis, steps):
@@ -47,13 +52,7 @@
     start_sums = [jnp.zeros((row_count, 3 * feature_width), jnp.float32)]
     start_sums = tuple(start_sums)
     own_cols = sources[0]
-    fresh = [
-        jnp.dot(
-            own_cols,
-            lax.all_gather(w_qkv, "fsdp", axis=0, tiled=True),
-            preferred_element_type=jnp.float32,
-        )
-    ]
+    fresh = [jnp.dot(own_cols, gather_over(w_qkv, "fsdp", 0), preferred_element_type=jnp.float32)]
     sums = tuple(fresh)
     packed = sums[0].astype(jnp.bfloat16)
     queries = packed[:, :feature_width]

time: 607 us -> 551 us (0.908)
  waiting for transfers between devices: 265 us -> 130 us
  blocking collectives: 0 us -> 78.7 us
    all_gather x1 -> x0, waiting for transfers between devices: 134 us -> none  [shards(): lax.all_gather(w_qkv, 'fsdp', axis=0, tiled=True)]
    all_to_all x0 -> x1, blocking collectives: none -> 78.7 us  [gather_over(): return jnp.concatenate(lax.all_to_all(sent, axis, 0, 0), axis=dim)]
  transfers between devices with their start and end apart: 4 -> 3, of which waited for: 3 -> 2; matrix products, arithmetic and copies ran while one was open for 47% -> 52% of each run, Pallas kernels for 0% -> 0%
where the time goes in v1:
time: 551 us; the launch traced here: 549 us
  local copies, waits for them, and re-layouts  191 us (35%)
  waiting for transfers between devices  130 us (24%)
  blocking collectives  78.7 us (14%)
  other arithmetic  64.4 us (12%)
  matrix products  63.9 us (12%)
  between operations  13.4 us (2%)
    ppermute x2, waiting for transfers between devices, from_behind(): return lax.ppermute(value, axis, pairs)  130 us
    all_to_all x1, blocking collectives, gather_over(): return jnp.concatenate(lax.all_to_all(sent, axis, 0, 0), axis=dim)  78.7 us
    slice x8, local copies, waits for them, and re-layouts, attend(): keyvals[..., :feature_width].reshape(block_count, -1, HEADS, head_width)  72.8 us
    concatenate x4, other arithmetic, attend(): keyvals = jnp.concatenate([own_blocks[:, None], picked], axis=1)  40.3 us
    gather x4, local copies, waits for them, and re-layouts, one_group(): picked = pool[layout_part]  39.9 us
    dot_general x4, matrix products, attend(): jnp.einsum('bhqk,bkhd->bqhd', rounded, value_heads, preferred_element_typ...  35.3 us
    slice x4, local copies, waits for them, and re-layouts, attend(): keyvals[..., feature_width:].reshape(block_count, -1, HEADS, head_width)  33.4 us
    while x16, local copies, waits for them, and re-layouts  21.4 us
  transfers between devices with their start and end apart: 3, of which 2 were waited for; matrix products, arithmetic and copies ran while one was open for 52% of the time, Pallas kernels for 0%

profile of v1, /device:TPU:1, one launch (start us, length us, event | category | flops | bytes accessed | tf_op | source)
XLA Modules:
  0.0 548.6 jit_solution(1069191660410699090)
XLA Ops:
  8.6 78.7 %all_to_all.5 = bf16[8,128,3072]{2,1,0:T(8,128)(2,1)S(1)} all-to-all(bf16[8,128,3072]{2,1,0:T(8,128)(2,1)S(1)} %stack.2), channel_id=1, replica_groups=mesh['seq'=16,'fsdp'=8] {'fsdp'}, dimensions={0} | all-to-all | bytes 12582912 | tf_op jit(solution)/shard_map/all_to_all | solution.py:14
  87.3 7.1 %convolution_convert_fusion = bf16[1024,3072]{1,0:T(8,128)(2,1)S(1)} fusion(bf16[1024,1024]{1,0:T(8,128)(2,1)S(1)} %copy-done, bf16[1024,3072]{1,0:T(8,128)(2,1)S(1)} %bitcast.80), kind=kOutput, calls=%fused_computation.36 | convolution fusion | flops 6445596672 | bytes 14680064 | tf_op jit(solution)/shard_map/dot_general | solution.py:55
  99.3 4.4 collective-permute-start
  106.9 126.8 %collective-permute-done = bf16[1024,2048]{1,0:T(8,128)(2,1)} collective-permute-done((bf16[1024,2048]{1,0:T(8,128)(2,1)}, bf16[1024,2048]{1,0:T(8,128)(2,1)}, u32[]{:S(2)}, u32[]{:S(2)}) %collective-permute-start) | collective-permute-done | bytes 4194336 | tf_op jit(solution)/shard_map/ppermute | solution.py:20
  236.6 11.3 %pad_maximum_fusion.1 = bf16[3072,2048]{1,0:T(8,128)(2,1)} fusion(bf16[1024,2048]{1,0:T(8,128)(2,1)} %collective-permute-done.1, bf16[1024,2048]{1,0:T(8,128)(2,1)} %slice.24, bf16[1024,2048]{1,0:T(8,128)(2,1)} %collective-permute-done), kind=kLoop, calls=%fused_computation.35 | loop fusion | flops 37748736 | bytes 25165824 | tf_op jit(solution)/shard_map/concatenate | solution.py:62
  247.9 287.8 %while.12 = (s32[]{:T(128)}, bf16[4,256,1024]{2,1,0:T(8,128)(2,1)}, s32[4]{0:T(128)S(1)}, bf16[24,128,2048]{2,1,0:T(8,128)(2,1)}, s32[4,2,10]{2,1,0:T(2,128)}, /...) while((s32[]{:T(128)}, bf16[4,256,1024]{2,1,0:T(8,128)(2,1)}, ...), condition=%wide.region_3.4_spmd, body=%wide.region_0.3_spmd.sunk | while | flops 1514416896 | bytes 190909680 | solution.py:75
  251.3 10.0 %gather_fusion = bf16[20,128,2048]{2,1,0:T(8,128)(2,1)} fusion(bf16[24,128,2048]{2,1,0:T(8,128)(2,1)} %get-tuple-element.200, s32[1024]{0:T(1024)S(1)} %pad_clamp_fusion.2), kind=kCustom, calls=%fused_computation.clone.1 | custom fusion | bytes 20971600 | tf_op jit(solution)/shard_map/while/body/eval_jaxpr/gather | solution.py:72
  261.3 10.1 %pad_maximum_fusion.3 = bf16[2,11,128,2048]{3,2,1,0:T(8,128)(2,1)} fusion(bf16[2,10,128,2048]{3,2,1,0:T(8,128)(2,1)} %bitcast.75, bf16[2,1,128,2048]{3,2,1,0:T(8,128)(2,1)S(1)} %dynamic-slice_bitcast_fusion.4), kind=kLoop, calls=%fused_computation.1.clone.1 | loop fusion | flops 5767168 | bytes 23068672 | tf_op jit(solution)/shard_map/while/body/eval_jaxpr/concatenate | solution.py:27
  271.3 9.9 %fusion.40 = (bf16[2,1408,1024]{2,1,0:T(8,128)(2,1)}, bf16[2,1408,1024]{2,1,0:T(8,128)(2,1)}) fusion(bf16[2,1408,2048]{2,1,0:T(8,128)(2,1)} %bitcast.73), kind=kLoop, calls=%fused_computation.38.clone.1 | loop fusion | bytes 23068672 | tf_op jit(solution)/shard_map/while/body/eval_jaxpr/slice | solution.py:29
  281.3 8.3 %copy.26 = bf16[2,1408,1024]{1,2,0:T(8,128)(2,1)} copy(bf16[2,1408,1024]{2,1,0:T(8,128)(2,1)} %get-tuple-element.170) | data formatting | bytes 11534336 | tf_op jit(solution)/shard_map/while/body/eval_jaxpr/slice | solution.py:29
  294.7 4.2 copy-done.2
  301.3 8.4 %copy.25 = bf16[2,1408,1024]{1,2,0:T(8,128)(2,1)} copy(bf16[2,1408,1024]{2,1,0:T(8,128)(2,1)} %get-tuple-element.169) | data formatting | bytes 11534336 | tf_op jit(solution)/shard_map/while/body/eval_jaxpr/slice | solution.py:30
  309.7 8.8 %divide_convert_fusion.2 = bf16[2,128,8,128]{1,3,2,0:T(8,128)(2,1)S(1)} fusion(bf16[2,1408,8,128]{1,3,2,0:T(8,128)(2,1)} %bitcast.77, f32[2,8,128,1408]{3,2,1,0:T(8,128)} %copy-done.2, f32[2,8,128]{2,1,0:T(8,128)S(1)} %get-tuple-element.172, pred[2,1408]{1,0:T(4,128)(4,1)S(1)} %broadcast_compare_fusion.2, f32[2,128,8]{1,2,0:T(8,128)S(1)} %bitcast.81), kind=kOutput, calls=%fused_computation.13.clone.1 | convolution fusion | flops 750256128 | bytes 17844992 | tf_op jit(solution)/shard_map/while/body/eval_jaxpr/bhqk,bkhd->bqhd/dot_general | solution.py:43
  323.2 10.0 %gather_fusion = bf16[20,128,2048]{2,1,0:T(8,128)(2,1)} fusion(bf16[24,128,2048]{2,1,0:T(8,128)(2,1)} %get-tuple-element.200, s32[1024]{0:T(1024)S(1)} %pad_clamp_fusion.2), kind=kCustom, calls=%fused_computation.clone.1 | custom fusion | bytes 20971600 | tf_op jit(solution)/shard_map/while/body/eval_jaxpr/gather | solution.py:72
  333.2 10.1 %pad_maximum_fusion.3 = bf16[2,11,128,2048]{3,2,1,0:T(8,128)(2,1)} fusion(bf16[2,10,128,2048]{3,2,1,0:T(8,128)(2,1)} %bitcast.75, bf16[2,1,128,2048]{3,2,1,0:T(8,128)(2,1)S(1)} %dynamic-slice_bitcast_fusion.4), kind=kLoop, calls=%fused_computation.1.clone.1 | loop fusion | flops 5767168 | bytes 23068672 | tf_op jit(solution)/shard_map/while/body/eval_jaxpr/concatenate | solution.py:27
  343.3 9.9 %fusion.40 = (bf16[2,1408,1024]{2,1,0:T(8,128)(2,1)}, bf16[2,1408,1024]{2,1,0:T(8,128)(2,1)}) fusion(bf16[2,1408,2048]{2,1,0:T(8,128)(2,1)} %bitcast.73), kind=kLoop, calls=%fused_computation.38.clone.1 | loop fusion | bytes 23068672 | tf_op jit(solution)/shard_map/while/body/eval_jaxpr/slice | solution.py:29
  353.2 8.3 %copy.26 = bf16[2,1408,1024]{1,2,0:T(8,128)(2,1)} copy(bf16[2,1408,1024]{2,1,0:T(8,128)(2,1)} %get-tuple-element.170) | data formatting | bytes 11534336 | tf_op jit(solution)/shard_map/while/body/eval_jaxpr/slice | solution.py:29
  373.3 8.4 %copy.25 = bf16[2,1408,1024]{1,2,0:T(8,128)(2,1)} copy(bf16[2,1408,1024]{2,1,0:T(8,128)(2,1)} %get-tuple-element.169) | data formatting | bytes 11534336 | tf_op jit(solution)/shard_map/while/body/eval_jaxpr/slice | solution.py:30
  381.6 8.8 %divide_convert_fusion.2 = bf16[2,128,8,128]{1,3,2,0:T(8,128)(2,1)S(1)} fusion(bf16[2,1408,8,128]{1,3,2,0:T(8,128)(2,1)} %bitcast.77, f32[2,8,128,1408]{3,2,1,0:T(8,128)} %copy-done.2, f32[2,8,128]{2,1,0:T(8,128)S(1)} %get-tuple-element.172, pred[2,1408]{1,0:T(4,128)(4,1)S(1)} %broadcast_compare_fusion.2, f32[2,128,8]{1,2,0:T(8,128)S(1)} %bitcast.81), kind=kOutput, calls=%fused_computation.13.clone.1 | convolution fusion | flops 750256128 | bytes 17844992 | tf_op jit(solution)/shard_map/while/body/eval_jaxpr/bhqk,bkhd->bqhd/dot_general | solution.py:43
  395.2 10.0 %gather_fusion = bf16[20,128,2048]{2,1,0:T(8,128)(2,1)} fusion(bf16[24,128,2048]{2,1,0:T(8,128)(2,1)} %get-tuple-element.200, s32[1024]{0:T(1024)S(1)} %pad_clamp_fusion.2), kind=kCustom, calls=%fused_computation.clone.1 | custom fusion | bytes 20971600 | tf_op jit(solution)/shard_map/while/body/eval_jaxpr/gather | solution.py:72
  405.2 10.1 %pad_maximum_fusion.3 = bf16[2,11,128,2048]{3,2,1,0:T(8,128)(2,1)} fusion(bf16[2,10,128,2048]{3,2,1,0:T(8,128)(2,1)} %bitcast.75, bf16[2,1,128,2048]{3,2,1,0:T(8,128)(2,1)S(1)} %dynamic-slice_bitcast_fusion.4), kind=kLoop, calls=%fused_computation.1.clone.1 | loop fusion | flops 5767168 | bytes 23068672 | tf_op jit(solution)/shard_map/while/body/eval_jaxpr/concatenate | solution.py:27
  415.3 9.9 %fusion.40 = (bf16[2,1408,1024]{2,1,0:T(8,128)(2,1)}, bf16[2,1408,1024]{2,1,0:T(8,128)(2,1)}) fusion(bf16[2,1408,2048]{2,1,0:T(8,128)(2,1)} %bitcast.73), kind=kLoop, calls=%fused_computation.38.clone.1 | loop fusion | bytes 23068672 | tf_op jit(solution)/shard_map/while/body/eval_jaxpr/slice | solution.py:29
  425.2 8.3 %copy.26 = bf16[2,1408,1024]{1,2,0:T(8,128)(2,1)} copy(bf16[2,1408,1024]{2,1,0:T(8,128)(2,1)} %get-tuple-element.170) | data formatting | bytes 11534336 | tf_op jit(solution)/shard_map/while/body/eval_jaxpr/slice | solution.py:29
  445.2 8.4 %copy.25 = bf16[2,1408,1024]{1,2,0:T(8,128)(2,1)} copy(bf16[2,1408,1024]{2,1,0:T(8,128)(2,1)} %get-tuple-element.169) | data formatting | bytes 11534336 | tf_op jit(solution)/shard_map/while/body/eval_jaxpr/slice | solution.py:30
  453.6 8.8 %divide_convert_fusion.2 = bf16[2,128,8,128]{1,3,2,0:T(8,128)(2,1)S(1)} fusion(bf16[2,1408,8,128]{1,3,2,0:T(8,128)(2,1)} %bitcast.77, f32[2,8,128,1408]{3,2,1,0:T(8,128)} %copy-done.2, f32[2,8,128]{2,1,0:T(8,128)S(1)} %get-tuple-element.172, pred[2,1408]{1,0:T(4,128)(4,1)S(1)} %broadcast_compare_fusion.2, f32[2,128,8]{1,2,0:T(8,128)S(1)} %bitcast.81), kind=kOutput, calls=%fused_computation.13.clone.1 | convolution fusion | flops 750256128 | bytes 17844992 | tf_op jit(solution)/shard_map/while/body/eval_jaxpr/bhqk,bkhd->bqhd/dot_general | solution.py:43
  467.1 10.0 %gather_fusion = bf16[20,128,2048]{2,1,0:T(8,128)(2,1)} fusion(bf16[24,128,2048]{2,1,0:T(8,128)(2,1)} %get-tuple-element.200, s32[1024]{0:T(1024)S(1)} %pad_clamp_fusion.2), kind=kCustom, calls=%fused_computation.clone.1 | custom fusion | bytes 20971600 | tf_op jit(solution)/shard_map/while/body/eval_jaxpr/gather | solution.py:72
  477.1 10.1 %pad_maximum_fusion.3 = bf16[2,11,128,2048]{3,2,1,0:T(8,128)(2,1)} fusion(bf16[2,10,128,2048]{3,2,1,0:T(8,128)(2,1)} %bitcast.75, bf16[2,1,128,2048]{3,2,1,0:T(8,128)(2,1)S(1)} %dynamic-slice_bitcast_fusion.4), kind=kLoop, calls=%fused_computation.1.clone.1 | loop fusion | flops 5767168 | bytes 23068672 | tf_op jit(solution)/shard_map/while/body/eval_jaxpr/concatenate | solution.py:27
  487.2 9.9 %fusion.40 = (bf16[2,1408,1024]{2,1,0:T(8,128)(2,1)}, bf16[2,1408,1024]{2,1,0:T(8,128)(2,1)}) fusion(bf16[2,1408,2048]{2,1,0:T(8,128)(2,1)} %bitcast.73), kind=kLoop, calls=%fused_computation.38.clone.1 | loop fusion | bytes 23068672 | tf_op jit(solution)/shard_map/while/body/eval_jaxpr/slice | solution.py:29
  497.1 8.3 %copy.26 = bf16[2,1408,1024]{1,2,0:T(8,128)(2,1)} copy(bf16[2,1408,1024]{2,1,0:T(8,128)(2,1)} %get-tuple-element.170) | data formatting | bytes 11534336 | tf_op jit(solution)/shard_map/while/body/eval_jaxpr/slice | solution.py:29
  517.2 8.4 %copy.25 = bf16[2,1408,1024]{1,2,0:T(8,128)(2,1)} copy(bf16[2,1408,1024]{2,1,0:T(8,128)(2,1)} %get-tuple-element.169) | data formatting | bytes 11534336 | tf_op jit(solution)/shard_map/while/body/eval_jaxpr/slice | solution.py:30
  525.5 8.8 %divide_convert_fusion.2 = bf16[2,128,8,128]{1,3,2,0:T(8,128)(2,1)S(1)} fusion(bf16[2,1408,8,128]{1,3,2,0:T(8,128)(2,1)} %bitcast.77, f32[2,8,128,1408]{3,2,1,0:T(8,128)} %copy-done.2, f32[2,8,128]{2,1,0:T(8,128)S(1)} %get-tuple-element.172, pred[2,1408]{1,0:T(4,128)(4,1)S(1)} %broadcast_compare_fusion.2, f32[2,128,8]{1,2,0:T(8,128)S(1)} %bitcast.81), kind=kOutput, calls=%fused_computation.13.clone.1 | convolution fusion | flops 750256128 | bytes 17844992 | tf_op jit(solution)/shard_map/while/body/eval_jaxpr/bhqk,bkhd->bqhd/dot_general | solution.py:43
  535.7 6.0 %convolution_convert_fusion.1 = bf16[1024,1024]{1,0:T(8,128)(2,1)} fusion(bf16[1024,1024]{1,0:T(8,128)(2,1)} %bitcast.83, bf16[1024,1024]{1,0:T(8,128)(2,1)} %all-gather.2.cloned.1.call-done), kind=kOutput, calls=%fused_computation.37 | convolution fusion | flops 2148532224 | bytes 6291456 | tf_op jit(solution)/shard_map/dot_general | solution.py:85
  (86 shorter events, 72.2 us)
Async XLA Ops:
  6.5 80.7 %copy-start = (bf16[1024,1024]{1,0:T(8,128)(2,1)S(1)}, bf16[1024,1024]{1,0:T(8,128)(2,1)}, u32[]{:S(2)}) copy-start(bf16[1024,1024]{1,0:T(8,128)(2,1)} %param.7) | copy-start | bytes 6291460
  6.5 529.2 %all-gather.2.cloned.1.call-start = ((), (), s32[]{:S(2)}) async-start(), calls=%async_computation.1 | async-start | bytes 2359296 | tf_op jit(solution)/shard_map/all_gather | solution.py:87
  94.4 2.7 copy-start.3
  97.0 6.7 %copy-start.4 = (s32[8]{0:T(128)S(1)}, s32[8]{0:T(128)}, u32[]{:S(2)}) copy-start(s32[8]{0:T(128)} %param.11) | copy-start | bytes 100
  99.3 134.4 %collective-permute-start = (bf16[1024,2048]{1,0:T(8,128)(2,1)}, bf16[1024,2048]{1,0:T(8,128)(2,1)}, u32[]{:S(2)}, u32[]{:S(2)}) collective-permute-start(bf16[1024,2048]{1,0:T(8,128)(2,1)} %slice.24), channel_id=1, source_target_pairs={{0,8},{8,16},{16,24},{24,32},{32,40},{40,48},{48,56},{56,64},{64,7... | collective-permute-start | bytes 12582920 | tf_op jit(solution)/shard_map/ppermute | solution.py:20
  103.7 132.9 %collective-permute-start.1 = (bf16[1024,2048]{1,0:T(8,128)(2,1)}, bf16[1024,2048]{1,0:T(8,128)(2,1)}, u32[]{:S(2)}, u32[]{:S(2)}) collective-permute-start(bf16[1024,2048]{1,0:T(8,128)(2,1)} %slice.24), channel_id=1, source_target_pairs={{0,120},{8,0},{16,8},{24,16},{32,24},{40,32},{48,40},{56,48},{64,5... | collective-permute-start | bytes 12582920 | tf_op jit(solution)/shard_map/ppermute | solution.py:20
  294.7 4.2 copy-start.2
  366.6 4.2 copy-start.2
  438.6 4.2 copy-start.2
  510.6 4.2 copy-start.2
  535.7 6.0 %copy-start.1 = (bf16[1024,1024]{1,0:T(8,128)(2,1)S(1)}, bf16[1024,1024]{1,0:T(8,128)(2,1)}, u32[]{:S(2)}) copy-start(bf16[1024,1024]{1,0:T(8,128)(2,1)} %param.7) | copy-start | bytes 6291460
Sparse Core Ops, SparseCore 0:
  103.8 108.8 all-gather.1
